TPU v7x, 256 devices: a whole 4x4x8 slice. The times are simulated.
256 devices in a mesh: pix: 64 (over z, y, core), band: 4 (over x).
Axes of the slice: x: 4, y: 4, z: 8, core: 2. Of those that a mesh axis runs over, the one named last changes fastest.
Arguments:
- series: bfloat16 [224, 128, 16384], P('band', None, 'pix'), may hold values from 0 to 1
- pixel_factor: float32 [64, 16384], P(None, 'pix'), may hold values from 0.03 to 0.6
- band_factor: float32 [224, 64], P('band'), may hold values from 0.03 to 0.6
- time_factor: float32 [128, 64], replicated, may hold values from 0.03 to 0.6
Outputs:
- pixels_out: float32 [64, 16384], P(None, 'pix')
- bands_out: float32 [224, 64], P('band')
- times_out: float32 [128, 64], replicated
All inputs are finite; a program needn't handle non-finite values.
Results may differ from a plain program's by a relative error of at most 0.00045.
Values sent between devices are 32-bit elements; how exact they have to be, the bound alone decides.
A program may use at most 64 MiB of HBM per device.

v0:
```python
import jax
import jax.numpy as jnp
from jax import lax
from jax.sharding import PartitionSpec as P

SWEEPS = 4
HIGH = lax.Precision.HIGHEST


def step_of(gram):
    return 1.0 / (jnp.max(jnp.sum(gram, axis=1)) + 1e-06)


def band_gram_of(bands):
    local_gram = jnp.dot(bands.T, bands, precision=HIGH, preferred_element_type=jnp.float32)
    return lax.psum(local_gram, "band")


def body(series, pixel_factor, band_factor, time_factor):
    pixels = pixel_factor
    bands = band_factor
    times = time_factor
    gram_b = band_gram_of(bands)
    for sweep in range(SWEEPS):
        gram_c = jnp.dot(times.T, times, precision=HIGH, preferred_element_type=jnp.float32)
        c_low = times.astype(jnp.bfloat16)
        folded = jnp.einsum("btp,tr->brp", series, c_low, preferred_element_type=jnp.float32)
        partial_a = jnp.einsum("brp,br->rp", folded, bands, precision=HIGH)
        gram = gram_b * gram_c
        scale = step_of(gram)
        target = lax.psum(partial_a, "band")
        pixels = jnp.maximum(pixels - scale * (jnp.dot(gram, pixels, precision=HIGH) - target), 0.0)
        local_gram = jnp.dot(pixels, pixels.T, precision=HIGH, preferred_element_type=jnp.float32)
        partial_b = jnp.einsum("brp,rp->br", folded, pixels, precision=HIGH)
        gram_a = lax.psum(local_gram, "pix")
        target_b = lax.psum(partial_b, "pix")
        gram = gram_a * gram_c
        bands = jnp.maximum(
            bands - step_of(gram) * (jnp.dot(bands, gram, precision=HIGH) - target_b), 0.0
        )
        gram_b = band_gram_of(bands)
        p_low = pixels.astype(jnp.bfloat16)
        b_low = bands.astype(jnp.bfloat16).astype(jnp.float32)
        spread = jnp.einsum("btp,rp->brt", series, p_low, preferred_element_type=jnp.float32)
        partial_c = jnp.einsum("brt,br->tr", spread, b_low, precision=HIGH)
        target_c = lax.psum(partial_c, ("pix", "band"))
        gram = gram_a * gram_b
        times = jnp.maximum(
            times - step_of(gram) * (jnp.dot(times, gram, precision=HIGH) - target_c), 0.0
        )
    return (pixels, bands, times)


def solution(mesh):
    placed = (P("band", None, "pix"), P(None, "pix"), P("band", None), P())
    return jax.shard_map(
        body,
        mesh=mesh,
        in_specs=placed,
        out_specs=(P(None, "pix"), P("band", None), P()),
        check_vma=False,
    )
```

profile of v0, /device:TPU:32, one launch (start us, length us, event | category | flops | bytes accessed | tf_op | source)
XLA Modules:
  0.0 1637.9 jit_solution(12999607043672692766)
XLA Ops:
  8.0 2.7 convolution_bitcast_fusion.3
  12.5 4.1 fusion.14
  17.8 17.1 %psum.147 = f32[64,64]{1,0:T(8,128)S(1)} all-reduce(f32[64,64]{1,0:T(8,128)S(1)} %fusion.102), channel_id=1, replica_groups=mesh['pix'=64,'band'=4] {'band'}, use_global_device_ids=true, to_apply=%region_0.0 | all-reduce | flops 4096 | bytes 32768 | tf_op jit(solution)/shard_map/psum | solution.py:16
  36.4 29.6 %all-reduce.9.cloned.1.call-done = f32[64,256]{1,0:T(8,128)} async-done(((f32[64,256]{1,0:T(8,128)}), f32[64,256]{1,0:T(8,128)}) %all-reduce.9.cloned.1.call-update) | async-done | bytes 65552 | tf_op jit(solution)/shard_map/psum | solution.py:31
  67.3 3.3 fusion.76
  70.6 4.9 fusion.12
  75.6 231.5 %all-reduce.3 = (f32[56,64]{1,0:T(8,128)S(1)}, f32[64,64]{0,1:T(8,128)S(1)}) all-reduce(f32[56,64]{1,0:T(8,128)S(1)} %bitcast.190, f32[64,64]{0,1:T(8,128)S(1)} %fusion.104), channel_id=1, replica_groups=mesh['pix'=64,'band'=4] {'pix'}, use_global_device_ids=true, to_apply=%region_7.0 | all-reduce | flops 7680 | bytes 61440 | tf_op jit(solution)/shard_map/psum | solution.py:36
  311.1 91.0 %psum.152 = f32[128,64]{0,1:T(8,128)S(1)} all-reduce(f32[128,64]{0,1:T(8,128)S(1)} %bitcast.186), channel_id=1, replica_groups=mesh['pix'=64,'band'=4] {'pix','band'}, use_global_device_ids=true, to_apply=%region_11.0 | all-reduce | flops 8192 | bytes 65536 | tf_op jit(solution)/shard_map/psum | solution.py:46
  402.1 15.7 psum.151
  419.3 2.7 convolution_bitcast_fusion.2
  423.8 4.1 fusion.10
  430.4 39.1 %all-reduce.11.cloned.1.call-done = f32[64,256]{1,0:T(8,128)} async-done(((f32[64,256]{1,0:T(8,128)}), f32[64,256]{1,0:T(8,128)}) %all-reduce.11.cloned.1.call-update) | async-done | bytes 65552 | tf_op jit(solution)/shard_map/psum | solution.py:31
  471.0 3.3 fusion.74
  474.3 4.9 fusion.8
  479.3 231.3 %all-reduce.2 = (f32[56,64]{1,0:T(8,128)S(1)}, f32[64,64]{0,1:T(8,128)S(1)}) all-reduce(f32[56,64]{1,0:T(8,128)S(1)} %bitcast.191, f32[64,64]{0,1:T(8,128)S(1)} %fusion.106), channel_id=1, replica_groups=mesh['pix'=64,'band'=4] {'pix'}, use_global_device_ids=true, to_apply=%region_18.0 | all-reduce | flops 7680 | bytes 61440 | tf_op jit(solution)/shard_map/psum | solution.py:36
  714.5 91.0 %psum.157 = f32[128,64]{0,1:T(8,128)S(1)} all-reduce(f32[128,64]{0,1:T(8,128)S(1)} %bitcast.187), channel_id=1, replica_groups=mesh['pix'=64,'band'=4] {'pix','band'}, use_global_device_ids=true, to_apply=%region_22.0 | all-reduce | flops 8192 | bytes 65536 | tf_op jit(solution)/shard_map/psum | solution.py:46
  805.5 16.0 psum.156
  823.0 2.7 convolution_bitcast_fusion.1
  827.4 4.1 fusion.6
  833.7 39.6 %all-reduce.13.cloned.1.call-done = f32[64,256]{1,0:T(8,128)} async-done(((f32[64,256]{1,0:T(8,128)}), f32[64,256]{1,0:T(8,128)}) %all-reduce.13.cloned.1.call-update) | async-done | bytes 65552 | tf_op jit(solution)/shard_map/psum | solution.py:31
  874.7 3.3 fusion.72
  878.0 4.9 fusion.4
  883.0 231.5 %all-reduce.1 = (f32[56,64]{1,0:T(8,128)S(1)}, f32[64,64]{0,1:T(8,128)S(1)}) all-reduce(f32[56,64]{1,0:T(8,128)S(1)} %bitcast.192, f32[64,64]{0,1:T(8,128)S(1)} %fusion.108), channel_id=1, replica_groups=mesh['pix'=64,'band'=4] {'pix'}, use_global_device_ids=true, to_apply=%region_29.0 | all-reduce | flops 7680 | bytes 61440 | tf_op jit(solution)/shard_map/psum | solution.py:36
  1118.5 91.0 %psum.162 = f32[128,64]{0,1:T(8,128)S(1)} all-reduce(f32[128,64]{0,1:T(8,128)S(1)} %bitcast.188), channel_id=1, replica_groups=mesh['pix'=64,'band'=4] {'pix','band'}, use_global_device_ids=true, to_apply=%region_33.0 | all-reduce | flops 8192 | bytes 65536 | tf_op jit(solution)/shard_map/psum | solution.py:46
  1209.5 15.7 psum.161
  1231.2 4.1 fusion.2
  1237.4 39.5 %all-reduce.15.cloned.1.call-done = f32[64,256]{1,0:T(8,128)} async-done(((f32[64,256]{1,0:T(8,128)}), f32[64,256]{1,0:T(8,128)}) %all-reduce.15.cloned.1.call-update) | async-done | bytes 65552 | tf_op jit(solution)/shard_map/psum | solution.py:31
  1278.4 3.3 fusion.70
  1281.7 4.9 fusion
  1286.7 231.6 %all-reduce = (f32[56,64]{1,0:T(8,128)S(1)}, f32[64,64]{0,1:T(8,128)S(1)}) all-reduce(f32[56,64]{1,0:T(8,128)S(1)} %bitcast.193, f32[64,64]{0,1:T(8,128)S(1)} %fusion.110), channel_id=1, replica_groups=mesh['pix'=64,'band'=4] {'pix'}, use_global_device_ids=true, to_apply=%region_40.0 | all-reduce | flops 7680 | bytes 61440 | tf_op jit(solution)/shard_map/psum | solution.py:36
  1522.1 91.0 %psum.167 = f32[128,64]{0,1:T(8,128)S(1)} all-reduce(f32[128,64]{0,1:T(8,128)S(1)} %bitcast.189), channel_id=1, replica_groups=mesh['pix'=64,'band'=4] {'pix','band'}, use_global_device_ids=true, to_apply=%region_44.0 | all-reduce | flops 8192 | bytes 65536 | tf_op jit(solution)/shard_map/psum | solution.py:46
  1613.1 15.7 psum.166
  (106 shorter events, 40.2 us)
Async XLA Ops:
  7.2 58.8 %all-reduce.9.cloned.1.call-start = ((), (), s32[]{:S(2)}) async-start(), calls=%async_computation | async-start | bytes 131072 | tf_op jit(solution)/shard_map/psum | solution.py:31
  10.7 1.8 copy-start
  12.5 4.8 copy-start.10
  12.5 5.0 copy-start.9
  12.5 53.4 %copy-start.12 = (f32[64,256]{1,0:T(8,128)S(1)}, f32[64,256]{1,0:T(8,128)}, u32[]{:S(2)}) copy-start(f32[64,256]{1,0:T(8,128)} %param.5) | copy-start | bytes 196612
  17.3 452.2 %all-reduce.11.cloned.1.call-start = ((), (), s32[]{:S(2)}) async-start(), calls=%async_computation.1 | async-start | bytes 131072 | tf_op jit(solution)/shard_map/psum | solution.py:31
  65.9 4.7 copy-start.1
  422.0 1.8 copy-start.2
  428.5 444.8 %all-reduce.13.cloned.1.call-start = ((), (), s32[]{:S(2)}) async-start(), calls=%async_computation.2 | async-start | bytes 131072 | tf_op jit(solution)/shard_map/psum | solution.py:31
  469.5 4.7 copy-start.3
  825.6 1.8 copy-start.4
  832.2 444.8 %all-reduce.15.cloned.1.call-start = ((), (), s32[]{:S(2)}) async-start(), calls=%async_computation.3 | async-start | bytes 131072 | tf_op jit(solution)/shard_map/psum | solution.py:31
  873.3 4.7 copy-start.5
  1229.4 1.8 copy-start.6
  1276.9 4.7 copy-start.7
  1278.2 8.4 copy-start.8
  1519.8 111.1 %copy-start.11 = (f32[56,64]{1,0:T(8,128)}, f32[56,64]{1,0:T(8,128)S(1)}, u32[]{:S(2)}) copy-start(f32[56,64]{1,0:T(8,128)S(1)} %fusion.55) | copy-start | bytes 43012
Sparse Core Ops, SparseCore 0:
  17.4 48.4 all-reduce.8
  428.6 40.8 all-reduce.10
  832.3 40.9 all-reduce.12
  1236.0 40.8 all-reduce.14
where the time goes:
time: 1650 us; the launch traced here: 1640 us
  blocking collectives  1370 us (83%)
  waiting for transfers between devices  148 us (9%)
  matrix products  77.5 us (5%)
  between operations  22.9 us (1%)
    psum x4, blocking collectives, body(): target_b = lax.psum(partial_b, 'pix')  926 us
    psum x4, blocking collectives, body(): target_c = lax.psum(partial_c, ('pix', 'band'))  364 us
    psum x4, waiting for transfers between devices, body(): target = lax.psum(partial_a, 'band')  148 us
    psum x5, blocking collectives, band_gram_of(): return lax.psum(local_gram, 'band')  80.2 us
  transfers between devices with their start and end apart: 4, of which 4 were waited for; matrix products, arithmetic and copies ran while one was open for 0% of the time, Pallas kernels for 0%

commit v1 on v0

--- a/solution.py
+++ b/solution.py
@@ -43,7 +43,8 @@
         b_low = bands.astype(jnp.bfloat16).astype(jnp.float32)
         spread = jnp.einsum("btp,rp->brt", series, p_low, preferred_element_type=jnp.float32)
         partial_c = jnp.einsum("brt,br->tr", spread, b_low, precision=HIGH)
-        target_c = lax.psum(partial_c, ("pix", "band"))
+        shards = lax.all_gather(partial_c, ("pix", "band"), axis=0, tiled=False)
+        target_c = shards.sum(axis=0)
         gram = gram_a * gram_b
         times = jnp.maximum(
             times - step_of(gram) * (jnp.dot(times, gram, precision=HIGH) - target_c), 0.0

time: 1650 us -> 1770 us (1.073)
  waiting for transfers between devices: 148 us -> 614 us
  blocking collectives: 1370 us -> 1010 us
  local copies, waits for them, and re-layouts: 11.6 us -> 33.3 us
    all_gather x0 -> x4, waiting for transfers between devices: none -> 454 us  [body(): shards = lax.all_gather(partial_c, ('pix', 'band'), axis=0, tiled=False)]
    psum x4 -> x0, blocking collectives: 364 us -> none  [body(): target_c = lax.psum(partial_c, ('pix', 'band'))]
    unnamed x27 -> x37, local copies, waits for them, and re-layouts: 8.02 us -> 29.8 us
  transfers between devices with their start and end apart: 4 -> 8, of which waited for: 4 -> 8; matrix products, arithmetic and copies ran while one was open for 0% -> 0% of each run, Pallas kernels for 0% -> 0%
where the time goes in v1:
time: 1770 us; the launch traced here: 1760 us
  blocking collectives  1010 us (57%)
  waiting for transfers between devices  614 us (35%)
  matrix products  73.8 us (4%)
  local copies, waits for them, and re-layouts  33.3 us (2%)
  between operations  23.3 us (1%)
    psum x4, blocking collectives, body(): target_b = lax.psum(partial_b, 'pix')  925 us
    all_gather x4, waiting for transfers between devices, body(): shards = lax.all_gather(partial_c, ('pix', 'band'), axis=0, tiled=False)  454 us
    psum x4, waiting for transfers between devices, body(): target = lax.psum(partial_a, 'band')  160 us
    psum x5, blocking collectives, band_gram_of(): return lax.psum(local_gram, 'band')  81.6 us
  transfers between devices with their start and end apart: 8, of which 8 were waited for; matrix products, arithmetic and copies ran while one was open for 0% of the time, Pallas kernels for 0%

profile of v1, /device:TPU:32, one launch (start us, length us, event | category | flops | bytes accessed | tf_op | source)
XLA Modules:
  0.0 1764.3 jit_solution(15109588421422133261)
XLA Ops:
  12.5 4.1 fusion.14
  17.8 17.1 psum.119
  36.4 29.6 %all-reduce.9.cloned.1.call-done = f32[64,256]{1,0:T(8,128)} async-done(((f32[64,256]{1,0:T(8,128)}), f32[64,256]{1,0:T(8,128)}) %all-reduce.9.cloned.1.call-update) | async-done | bytes 65552 | tf_op jit(solution)/shard_map/psum | solution.py:31
  67.3 3.3 fusion.76
  70.6 4.9 fusion.12
  75.6 231.5 %all-reduce.3 = (f32[56,64]{1,0:T(8,128)S(1)}, f32[64,64]{0,1:T(8,128)S(1)}) all-reduce(f32[56,64]{1,0:T(8,128)S(1)} %bitcast.214, f32[64,64]{0,1:T(8,128)S(1)} %fusion.104), channel_id=1, replica_groups=mesh['pix'=64,'band'=4] {'pix'}, use_global_device_ids=true, to_apply=%region_7.0 | all-reduce | flops 7680 | bytes 61440 | tf_op jit(solution)/shard_map/psum | solution.py:36
  311.8 16.0 psum.123
  329.1 113.5 %all-gather.9.cloned.1.call-done = f32[32768,64]{0,1:T(8,128)} async-done(((f32[128,64]{0,1:T(8,128)}), f32[32768,64]{0,1:T(8,128)}) %all-gather.9.cloned.1.call-update) | async-done | bytes 8388624 | tf_op jit(solution)/shard_map/all_gather | solution.py:46
  442.6 4.9 copy.65
  451.9 4.1 fusion.10
  458.6 43.4 %all-reduce.11.cloned.1.call-done = f32[64,256]{1,0:T(8,128)} async-done(((f32[64,256]{1,0:T(8,128)}), f32[64,256]{1,0:T(8,128)}) %all-reduce.11.cloned.1.call-update) | async-done | bytes 65552 | tf_op jit(solution)/shard_map/psum | solution.py:31
  503.4 3.3 fusion.74
  506.7 4.9 fusion.8
  511.7 231.3 %all-reduce.2 = (f32[56,64]{1,0:T(8,128)S(1)}, f32[64,64]{0,1:T(8,128)S(1)}) all-reduce(f32[56,64]{1,0:T(8,128)S(1)} %bitcast.215, f32[64,64]{0,1:T(8,128)S(1)} %fusion.106), channel_id=1, replica_groups=mesh['pix'=64,'band'=4] {'pix'}, use_global_device_ids=true, to_apply=%region_18.0 | all-reduce | flops 7680 | bytes 61440 | tf_op jit(solution)/shard_map/psum | solution.py:36
  747.6 16.2 psum.127
  765.2 113.2 %all-gather.11.cloned.1.call-done = f32[32768,64]{0,1:T(8,128)} async-done(((f32[128,64]{0,1:T(8,128)}), f32[32768,64]{0,1:T(8,128)}) %all-gather.11.cloned.1.call-update) | async-done | bytes 8388624 | tf_op jit(solution)/shard_map/all_gather | solution.py:46
  878.5 4.9 copy.66
  887.8 4.1 fusion.6
  894.3 43.5 %all-reduce.13.cloned.1.call-done = f32[64,256]{1,0:T(8,128)} async-done(((f32[64,256]{1,0:T(8,128)}), f32[64,256]{1,0:T(8,128)}) %all-reduce.13.cloned.1.call-update) | async-done | bytes 65552 | tf_op jit(solution)/shard_map/psum | solution.py:31
  939.3 3.3 fusion.72
  942.6 4.9 fusion.4
  947.6 231.3 %all-reduce.1 = (f32[56,64]{1,0:T(8,128)S(1)}, f32[64,64]{0,1:T(8,128)S(1)}) all-reduce(f32[56,64]{1,0:T(8,128)S(1)} %bitcast.216, f32[64,64]{0,1:T(8,128)S(1)} %fusion.108), channel_id=1, replica_groups=mesh['pix'=64,'band'=4] {'pix'}, use_global_device_ids=true, to_apply=%region_29.0 | all-reduce | flops 7680 | bytes 61440 | tf_op jit(solution)/shard_map/psum | solution.py:36
  1183.5 16.3 psum.131
  1201.2 113.1 %all-gather.13.cloned.1.call-done = f32[32768,64]{0,1:T(8,128)} async-done(((f32[128,64]{0,1:T(8,128)}), f32[32768,64]{0,1:T(8,128)}) %all-gather.13.cloned.1.call-update) | async-done | bytes 8388624 | tf_op jit(solution)/shard_map/all_gather | solution.py:46
  1314.3 4.9 copy.67
  1323.7 4.1 fusion.2
  1330.3 43.5 %all-reduce.15.cloned.1.call-done = f32[64,256]{1,0:T(8,128)} async-done(((f32[64,256]{1,0:T(8,128)}), f32[64,256]{1,0:T(8,128)}) %all-reduce.15.cloned.1.call-update) | async-done | bytes 65552 | tf_op jit(solution)/shard_map/psum | solution.py:31
  1378.5 4.9 fusion
  1383.5 231.3 %all-reduce = (f32[56,64]{1,0:T(8,128)S(1)}, f32[64,64]{0,1:T(8,128)S(1)}) all-reduce(f32[56,64]{1,0:T(8,128)S(1)} %bitcast.217, f32[64,64]{0,1:T(8,128)S(1)} %fusion.110), channel_id=1, replica_groups=mesh['pix'=64,'band'=4] {'pix'}, use_global_device_ids=true, to_apply=%region_40.0 | all-reduce | flops 7680 | bytes 61440 | tf_op jit(solution)/shard_map/psum | solution.py:36
  1619.3 16.0 psum.135
  1636.5 113.7 %all-gather.15.cloned.1.call-done = f32[32768,64]{0,1:T(8,128)} async-done(((f32[128,64]{0,1:T(8,128)}), f32[32768,64]{0,1:T(8,128)}) %all-gather.15.cloned.1.call-update) | async-done | bytes 8388624 | tf_op jit(solution)/shard_map/all_gather | solution.py:46
  1750.2 4.9 copy.68
  (128 shorter events, 55.1 us)
Async XLA Ops:
  7.2 58.8 %all-reduce.9.cloned.1.call-start = ((), (), s32[]{:S(2)}) async-start(), calls=%async_computation | async-start | bytes 131072 | tf_op jit(solution)/shard_map/psum | solution.py:31
  10.7 1.8 copy-start.3
  12.5 4.8 copy-start.13
  12.5 5.0 copy-start.12
  12.5 53.4 %copy-start.15 = (f32[64,256]{1,0:T(8,128)S(1)}, f32[64,256]{1,0:T(8,128)}, u32[]{:S(2)}) copy-start(f32[64,256]{1,0:T(8,128)} %param.5) | copy-start | bytes 196612
  17.3 425.3 %all-gather.9.cloned.1.call-start = ((), (), s32[]{:S(2)}) async-start(), calls=%async_computation.4 | async-start | bytes 8421376 | tf_op jit(solution)/shard_map/all_gather | solution.py:46
  65.9 4.7 copy-start.4
  311.4 190.6 %all-reduce.11.cloned.1.call-start = ((), (), s32[]{:S(2)}) async-start(), calls=%async_computation.1 | async-start | bytes 131072 | tf_op jit(solution)/shard_map/psum | solution.py:31
  447.4 2.0 copy-start
  450.1 1.8 copy-start.5
  456.7 421.8 %all-gather.11.cloned.1.call-start = ((), (), s32[]{:S(2)}) async-start(), calls=%async_computation.5 | async-start | bytes 8421376 | tf_op jit(solution)/shard_map/all_gather | solution.py:46
  502.0 4.7 copy-start.6
  747.3 190.6 %all-reduce.13.cloned.1.call-start = ((), (), s32[]{:S(2)}) async-start(), calls=%async_computation.2 | async-start | bytes 131072 | tf_op jit(solution)/shard_map/psum | solution.py:31
  883.3 2.0 copy-start.1
  886.0 1.8 copy-start.7
  892.5 421.8 %all-gather.13.cloned.1.call-start = ((), (), s32[]{:S(2)}) async-start(), calls=%async_computation.6 | async-start | bytes 8421376 | tf_op jit(solution)/shard_map/all_gather | solution.py:46
  937.8 4.7 copy-start.8
  1183.1 190.6 %all-reduce.15.cloned.1.call-start = ((), (), s32[]{:S(2)}) async-start(), calls=%async_computation.3 | async-start | bytes 131072 | tf_op jit(solution)/shard_map/psum | solution.py:31
  1319.2 2.0 copy-start.2
  1321.9 1.8 copy-start.9
  1328.4 421.8 %all-gather.15.cloned.1.call-start = ((), (), s32[]{:S(2)}) async-start(), calls=%async_computation.7 | async-start | bytes 8421376 | tf_op jit(solution)/shard_map/all_gather | solution.py:46
  1373.7 4.7 copy-start.10
  1375.0 8.4 copy-start.11
  1616.3 138.8 %copy-start.14 = (f32[56,64]{1,0:T(8,128)}, f32[56,64]{1,0:T(8,128)S(1)}, u32[]{:S(2)}) copy-start(f32[56,64]{1,0:T(8,128)S(1)} %fusion.55) | copy-start | bytes 43012
Sparse Core Ops, SparseCore 0:
  17.4 48.4 all-reduce.8
  311.5 131.0 all-gather.8
  456.8 45.1 all-reduce.10
  747.4 131.0 all-gather.10
  892.7 45.1 all-reduce.12
  1183.3 131.0 all-gather.12
  1328.5 45.1 all-reduce.14
  1619.2 131.0 all-gather.14
